TPU v7x, 32 devices: a whole 2x2x4 slice. The times are simulated.
32 devices in a mesh: half: 1, grp: 4 (over y, core), dev: 8 (over z, x).
Axes of the slice: x: 2, y: 2, z: 4, core: 2. Of those that a mesh axis runs over, the one named last changes fastest.
Arguments:
- panel_block: float32 [2048, 512], P(('half', 'grp', 'dev')), may hold values from -1 to 1, as said below
- trailing: float32 [2048, 1024], P(('half', 'grp'), 'dev'), may hold values from -6 to 6
Outputs:
- triangle: float32 [512, 512], replicated
- projected: float32 [512, 1024], P(None, 'dev')
- remainder: float32 [2048, 1024], P(('half', 'grp'), 'dev')
Inputs may be any that keep to these rules, and one draw needn't show every extreme that they name: `panel_block`: of full column rank.
All inputs are finite; a program needn't handle non-finite values.
Results may differ from a plain program's by a relative error of at most 0.0003.
Values sent between devices are 32-bit elements; how exact they have to be, the bound alone decides.
A program may use at most 64 MiB of HBM per device.

v0:
```python
import jax
import jax.numpy as jnp
from jax import lax
from jax.sharding import PartitionSpec as P


def on_device(panel_block, trailing):
    highest = lax.Precision.HIGHEST
    panel_group = lax.all_gather(panel_block, "dev", axis=0, tiled=True)
    gram_part = jnp.dot(panel_group.T, panel_group, precision=highest)
    cross_part = jnp.dot(panel_group.T, trailing, precision=highest)
    gram_sum, cross_sum = lax.psum((gram_part, cross_part), ("half", "grp"))
    factor = jnp.linalg.cholesky(gram_sum)
    projected = lax.linalg.triangular_solve(factor, cross_sum, left_side=True, lower=True)
    solved = lax.linalg.triangular_solve(
        factor, projected, left_side=True, lower=True, transpose_a=True
    )
    remainder = trailing - jnp.dot(panel_group, solved, precision=highest)
    triangle = factor.T
    return (triangle, projected, remainder)


def solution(mesh):
    placed = (P(("half", "grp", "dev"), None), P(("half", "grp"), "dev"))
    return jax.shard_map(
        on_device,
        mesh=mesh,
        in_specs=placed,
        out_specs=(P(), P(None, "dev"), P(("half", "grp"), "dev")),
        check_vma=False,
    )
```

profile of v0, /device:TPU:0, one launch (start us, length us, event | category | flops | bytes accessed | tf_op | source)
XLA Modules:
  0.0 260.0 jit_solution(11239562665385252636)
XLA Ops:
  7.2 0.7 all-gather.2.cloned.1.call-update
  8.0 45.2 %all-gather.2.cloned.1.call-done = f32[512,512]{1,0:T(8,128)} async-done(((f32[64,512]{1,0:T(8,128)}), f32[512,512]{1,0:T(8,128)}) %all-gather.2.cloned.1.call-update) | async-done | bytes 1048592 | tf_op jit(solution)/shard_map/all_gather | solution.py:9
  53.1 4.5 %fusion.59 = f32[512,512]{0,1:T(8,128)} fusion(f32[512,512]{1,0:T(8,128)} %all-gather.2.cloned.1.call-done), kind=kOutput, calls=%fused_computation.99 | convolution fusion | flops 1610612736 | bytes 2097152 | tf_op jit(solution)/shard_map/dot_general | solution.py:10
  57.6 2.5 fusion.60
  60.3 37.8 %all-reduce.4.cloned.1.call-done = (f32[512,512]{0,1:T(8,128)}, f32[512,128]{1,0:T(8,128)}) async-done(((f32[512,512]{0,1:T(8,128)}, f32[512,128]{1,0:T(8,128)}), (f32[512,512]{0,1:T(8,128)}, f32[512,128]{1,0:T(8,128)})) %all-reduce.4.cloned.1.call-update) | async-done | bytes 1310736 | tf_op jit(solution)/shard_map/psum | solution.py:12
  98.2 1.6 copy.6
  100.1 1.0 copy-done.3
  101.0 11.7 %cholesky.104 = f32[128,128]{1,0:T(8,128)S(1)} custom-call(f32[128,128]{1,0:T(8,128)S(1)} %cholesky.266), custom_call_target="Cholesky" | custom-call | tf_op jit(solution)/shard_map/jit(cholesky)/cholesky | solution.py:13
  112.8 9.8 %custom-call.32 = f32[1,128,128]{1,2,0:T(8,128)S(1)} custom-call(f32[1,128,128]{2,1,0:T(8,128)S(1)} %get-tuple-element.37), custom_call_target="InvertDiagBlocksLowerTriangular" | custom-call | tf_op jit(solution)/shard_map/jit(cholesky)/cholesky | solution.py:13
  123.4 0.7 copy-done.6
  124.1 11.9 %cholesky.217 = f32[128,128]{1,0:T(8,128)S(1)} custom-call(f32[128,128]{1,0:T(8,128)S(1)} %cholesky.270), custom_call_target="Cholesky" | custom-call | tf_op jit(solution)/shard_map/jit(cholesky)/cholesky | solution.py:13
  136.0 9.8 %custom-call.33 = f32[1,128,128]{1,2,0:T(8,128)S(1)} custom-call(f32[1,128,128]{2,1,0:T(8,128)S(1)} %get-tuple-element.34), custom_call_target="InvertDiagBlocksLowerTriangular" | custom-call | tf_op jit(solution)/shard_map/jit(cholesky)/cholesky | solution.py:13
  145.8 1.2 convolution_dynamic-update-slice_fusion
  148.0 13.2 %cholesky.238 = f32[128,128]{1,0:T(8,128)} custom-call(f32[128,128]{1,0:T(8,128)} %cholesky.275), custom_call_target="Cholesky" | custom-call | tf_op jit(solution)/shard_map/jit(cholesky)/cholesky | solution.py:13
  161.2 1.5 select_reduce_fusion.1
  162.7 0.7 compare_reduce_fusion.1
  163.4 11.3 %custom-call.34 = f32[1,128,128]{1,2,0:T(8,128)} custom-call(f32[1,128,128]{2,1,0:T(8,128)} %get-tuple-element.31), custom_call_target="InvertDiagBlocksLowerTriangular" | custom-call | tf_op jit(solution)/shard_map/jit(cholesky)/cholesky | solution.py:13
  174.7 1.0 convolution_dynamic-update-slice_fusion.1
  176.1 11.9 %cholesky.255 = f32[128,128]{1,0:T(8,128)S(1)} custom-call(f32[128,128]{1,0:T(8,128)S(1)} %convolution_subtract_fusion.8), custom_call_target="Cholesky" | custom-call | tf_op jit(solution)/shard_map/jit(cholesky)/cholesky | solution.py:13
  188.6 0.6 compare_reduce_fusion.2
  191.8 1.2 fusion.2
  193.1 10.9 %while.1 = (s32[]{:T(128)}, f32[512,512]{1,0:T(8,128)S(1)}, s32[4,2]{0,1:T(2,128)S(1)}, f32[4,128,128]{2,1,0:T(8,128)}, s32[]{:T(128)}) while((s32[]{:T(128)}, f32[512,512]{1,0:T(8,128)S(1)}, s32[4,2]{0,1:T(2,128)S(1)}, f32[4,128,128]{2,1,0:T(8,128)}, s32[]{:T(128)}) %tuple.33), condition=%wide.while_cond, body=%wide.while_body.sunk | while | flops 2 | bytes 132705 | solution.py:14
  193.7 2.1 bitcast_dynamic-update-slice_fusion.2
  196.5 2.1 bitcast_dynamic-update-slice_fusion.2
  199.2 2.1 bitcast_dynamic-update-slice_fusion.2
  201.9 2.1 bitcast_dynamic-update-slice_fusion.2
  204.0 40.1 %custom-call.35 = f32[4,128,128]{1,2,0:T(8,128)S(1)} custom-call(f32[4,128,128]{2,1,0:T(8,128)} %get-tuple-element.10), custom_call_target="InvertDiagBlocksLowerTriangular" | custom-call | tf_op jit(solution)/shard_map/triangular_solve | solution.py:14
  244.1 1.1 fusion.39
  247.2 0.7 pad_maximum_fusion
  249.7 1.3 fusion
  251.0 0.8 copy.9
  251.8 1.3 copy.8
  (55 shorter events, 9.7 us)
Async XLA Ops:
  7.2 46.0 %all-gather.2.cloned.1.call-start = ((), (), s32[]{:S(2)}) async-start(), calls=%async_computation | async-start | bytes 1179648 | tf_op jit(solution)/shard_map/all_gather | solution.py:9
  7.9 49.7 %copy-start.5 = (f32[512,128]{1,0:T(8,128)S(1)}, f32[512,128]{1,0:T(8,128)}, u32[]{:S(2)}) copy-start(f32[512,128]{1,0:T(8,128)} %param.3) | copy-start | bytes 786436
  7.9 90.2 %all-reduce.4.cloned.1.call-start = ((), (), s32[]{:S(2)}) async-start(), calls=%async_computation.1 | async-start | bytes 2621440 | tf_op jit(solution)/shard_map/psum | solution.py:12
  53.1 4.5 %copy-start = (f32[512,512]{1,0:T(8,128)S(1)}, f32[512,512]{1,0:T(8,128)}, u32[]{:S(2)}) copy-start(f32[512,512]{1,0:T(8,128)} %all-gather.2.cloned.1.call-done) | copy-start | bytes 3145732
  98.2 1.7 copy-start.1
  100.0 1.0 copy-start.3
  101.0 21.7 %copy-start.4 = (f32[512,512]{1,0:T(8,128)S(1)}, f32[512,512]{1,0:T(8,128)}, u32[]{:S(2)}) copy-start(f32[512,512]{1,0:T(8,128)} %copy-done.3) | copy-start | bytes 3145732
  123.4 0.7 copy-start.6
  193.1 52.2 %copy-start.7 = (f32[512,128]{1,0:T(8,128)S(1)}, f32[512,128]{1,0:T(8,128)}, u32[]{:S(2)}) copy-start(f32[512,128]{1,0:T(8,128)} %get-tuple-element.23) | copy-start | bytes 786436
  249.7 2.1 copy-start.2
Sparse Core Ops, SparseCore 0:
  10.1 42.9 all-gather.1
  60.3 37.8 all-reduce.3
where the time goes:
time: 261 us; the launch traced here: 260 us
  other arithmetic  125 us (48%)
  waiting for transfers between devices  83.7 us (32%)
  local copies, waits for them, and re-layouts  17.3 us (7%)
  between operations  16.9 us (6%)
  matrix products  16.6 us (6%)
    another operation x14, other arithmetic, on_device(): factor = jnp.linalg.cholesky(gram_sum)  83.1 us
    all_gather x1, waiting for transfers between devices, on_device(): panel_group = lax.all_gather(panel_block, 'dev', axis=0, tiled=True)  45.2 us
    another operation x4, other arithmetic, on_device(): lax.linalg.triangular_solve(factor, cross_sum, left_side=True, lower=True)  42.1 us
    psum x1, waiting for transfers between devices, on_device(): gram_sum, cross_sum = lax.psum((gram_part, cross_part), ('half', 'grp'))  37.8 us
    another operation x12, local copies, waits for them, and re-layouts  10.9 us
  transfers between devices with their start and end apart: 2, of which 2 were waited for; matrix products, arithmetic and copies ran while one was open for 0% of the time, Pallas kernels for 0%

commit v1 on v0

--- a/solution.py
+++ b/solution.py
@@ -6,7 +6,27 @@
 
 def on_device(panel_block, trailing):
     highest = lax.Precision.HIGHEST
-    panel_group = lax.all_gather(panel_block, "dev", axis=0, tiled=True)
+
+    def create_the_arrays(array_here, array_dim):
+        lane_axis = "dev"
+        width = lax.psum(1, lane_axis)
+        buffer = tuple(((j0, (j0 + 1) % width) for j0 in range(width)))
+
+        def unite_the_positions(z1):
+            if len(z1) == width:
+                return z1
+            after = lax.ppermute(z1[0], lane_axis, buffer)
+            piece_next = unite_the_positions([after, *z1])
+            return piece_next
+
+        main = unite_the_positions([array_here])
+        oldest = jnp.concatenate(main, array_dim)
+        kept_arr = jnp.roll(
+            oldest, (lax.axis_index(lane_axis) + 1) * array_here.shape[array_dim], array_dim
+        )
+        return kept_arr
+
+    panel_group = create_the_arrays(panel_block, 0)
     gram_part = jnp.dot(panel_group.T, panel_group, precision=highest)
     cross_part = jnp.dot(panel_group.T, trailing, precision=highest)
     gram_sum, cross_sum = lax.psum((gram_part, cross_part), ("half", "grp"))

time: 261 us -> 276 us (1.057)
  waiting for transfers between devices: 83.7 us -> 90.9 us
  matrix products: 16.6 us -> 21.8 us
  other arithmetic: 125 us -> 122 us
  starting transfers between devices: 0.08 us -> 3.07 us
    ppermute x0 -> x7, waiting for transfers between devices: none -> 54 us  [unite_the_positions(): after = lax.ppermute(z1[0], lane_axis, buffer)]
    all_gather x1 -> x0, waiting for transfers between devices: 45.2 us -> none  [on_device(): panel_group = lax.all_gather(panel_block, 'dev', axis=0, tiled=True)]
    another operation x14, other arithmetic: 83.1 us -> 78.6 us  [on_device(): factor = jnp.linalg.cholesky(gram_sum)]
    ppermute x0 -> x7, starting transfers between devices: none -> 3.04 us  [unite_the_positions(): after = lax.ppermute(z1[0], lane_axis, buffer)]
    another operation x12, local copies, waits for them, and re-layouts: 10.9 us -> 13.7 us
  transfers between devices with their start and end apart: 2 -> 8, of which waited for: 2 -> 8; matrix products, arithmetic and copies ran while one was open for 0% -> 0% of each run, Pallas kernels for 0% -> 0%
where the time goes in v1:
time: 276 us; the launch traced here: 275 us
  other arithmetic  122 us (44%)
  waiting for transfers between devices  90.9 us (33%)
  matrix products  21.8 us (8%)
  local copies, waits for them, and re-layouts  19.9 us (7%)
  between operations  17.2 us (6%)
  starting transfers between devices  3.07 us (1%)
    another operation x14, other arithmetic, on_device(): factor = jnp.linalg.cholesky(gram_sum)  78.6 us
    ppermute x7, waiting for transfers between devices, unite_the_positions(): after = lax.ppermute(z1[0], lane_axis, buffer)  54 us
    another operation x4, other arithmetic, on_device(): lax.linalg.triangular_solve(factor, cross_sum, left_side=True, lower=True)  42.4 us
    psum x1, waiting for transfers between devices, on_device(): gram_sum, cross_sum = lax.psum((gram_part, cross_part), ('half', 'grp'))  36.9 us
    another operation x12, local copies, waits for them, and re-layouts  13.7 us
  transfers between devices with their start and end apart: 8, of which 8 were waited for; matrix products, arithmetic and copies ran while one was open for 0% of the time, Pallas kernels for 0%

profile of v1, /device:TPU:0, one launch (start us, length us, event | category | flops | bytes accessed | tf_op | source)
XLA Modules:
  0.0 275.4 jit_solution(13586894433757514804)
XLA Ops:
  7.2 3.0 %collective-permute-start = (f32[64,512]{1,0:T(8,128)}, f32[64,512]{1,0:T(8,128)S(1)}, u32[]{:S(2)}, u32[]{:S(2)}) collective-permute-start(f32[64,512]{1,0:T(8,128)} %param.2), channel_id=1, source_target_pairs={{0,1},{1,2},{2,3},{3,4},{4,5},{5,6},{6,7},{7,0},{8,9},{9,10},{10,1... | collective-permute-start | bytes 393224 | tf_op jit(solution)/shard_map/ppermute | solution.py:18
  10.2 6.7 %collective-permute-done = f32[64,512]{1,0:T(8,128)S(1)} collective-permute-done((f32[64,512]{1,0:T(8,128)}, f32[64,512]{1,0:T(8,128)S(1)}, u32[]{:S(2)}, u32[]{:S(2)}) %collective-permute-start) | collective-permute-done | bytes 131104 | tf_op jit(solution)/shard_map/ppermute | solution.py:18
  17.0 7.7 %collective-permute-done.1 = f32[64,512]{1,0:T(8,128)S(1)} collective-permute-done((f32[64,512]{1,0:T(8,128)S(1)}, f32[64,512]{1,0:T(8,128)S(1)}, u32[]{:S(2)}, u32[]{:S(2)}) %collective-permute-start.1) | collective-permute-done | bytes 131104 | tf_op jit(solution)/shard_map/ppermute | solution.py:18
  24.7 7.7 %collective-permute-done.2 = f32[64,512]{1,0:T(8,128)S(1)} collective-permute-done((f32[64,512]{1,0:T(8,128)S(1)}, f32[64,512]{1,0:T(8,128)S(1)}, u32[]{:S(2)}, u32[]{:S(2)}) %collective-permute-start.2) | collective-permute-done | bytes 131104 | tf_op jit(solution)/shard_map/ppermute | solution.py:18
  32.3 7.7 %collective-permute-done.3 = f32[64,512]{1,0:T(8,128)S(1)} collective-permute-done((f32[64,512]{1,0:T(8,128)S(1)}, f32[64,512]{1,0:T(8,128)S(1)}, u32[]{:S(2)}, u32[]{:S(2)}) %collective-permute-start.3) | collective-permute-done | bytes 131104 | tf_op jit(solution)/shard_map/ppermute | solution.py:18
  40.0 7.7 %collective-permute-done.4 = f32[64,512]{1,0:T(8,128)S(1)} collective-permute-done((f32[64,512]{1,0:T(8,128)S(1)}, f32[64,512]{1,0:T(8,128)S(1)}, u32[]{:S(2)}, u32[]{:S(2)}) %collective-permute-start.4) | collective-permute-done | bytes 131104 | tf_op jit(solution)/shard_map/ppermute | solution.py:18
  47.7 8.9 %collective-permute-done.5 = f32[64,512]{1,0:T(8,128)S(1)} collective-permute-done((f32[64,512]{1,0:T(8,128)S(1)}, f32[64,512]{1,0:T(8,128)S(1)}, u32[]{:S(2)}, u32[]{:S(2)}) %collective-permute-start.5) | collective-permute-done | bytes 131104 | tf_op jit(solution)/shard_map/ppermute | solution.py:18
  56.6 7.7 %collective-permute-done.6 = f32[64,512]{1,0:T(8,128)S(1)} collective-permute-done((f32[64,512]{1,0:T(8,128)S(1)}, f32[64,512]{1,0:T(8,128)S(1)}, u32[]{:S(2)}, u32[]{:S(2)}) %collective-permute-start.6) | collective-permute-done | bytes 131104 | tf_op jit(solution)/shard_map/ppermute | solution.py:18
  65.4 2.9 %fusion.5 = f32[512,512]{0,1:T(8,128)} fusion(f32[1024,512]{1,0:T(8,128)S(1)} %constant_dynamic-update-slice_fusion, s32[]{:T(128)S(6)} %select_n.18), kind=kOutput, calls=%fused_computation.22 | convolution fusion | flops 1610612736 | bytes 2097156 | tf_op jit(solution)/shard_map/dot_general | solution.py:30
  68.3 2.5 fusion.3
  70.9 36.9 %all-reduce.4.cloned.1.call-done = (f32[512,512]{0,1:T(8,128)}, f32[512,128]{1,0:T(8,128)}) async-done(((f32[512,512]{0,1:T(8,128)}, f32[512,128]{1,0:T(8,128)}), (f32[512,512]{0,1:T(8,128)}, f32[512,128]{1,0:T(8,128)})) %all-reduce.4.cloned.1.call-update) | async-done | bytes 1310736 | tf_op jit(solution)/shard_map/psum | solution.py:32
  107.8 2.6 copy.6
  110.4 1.4 fusion
  112.8 11.7 %cholesky.104 = f32[128,128]{1,0:T(8,128)S(1)} custom-call(f32[128,128]{1,0:T(8,128)S(1)} %cholesky.266), custom_call_target="Cholesky" | custom-call | tf_op jit(solution)/shard_map/jit(cholesky)/cholesky | solution.py:33
  124.7 9.8 %custom-call.32 = f32[1,128,128]{1,2,0:T(8,128)S(1)} custom-call(f32[1,128,128]{2,1,0:T(8,128)S(1)} %get-tuple-element.37), custom_call_target="InvertDiagBlocksLowerTriangular" | custom-call | tf_op jit(solution)/shard_map/jit(cholesky)/cholesky | solution.py:33
  137.1 11.9 %cholesky.217 = f32[128,128]{1,0:T(8,128)S(1)} custom-call(f32[128,128]{1,0:T(8,128)S(1)} %cholesky.270), custom_call_target="Cholesky" | custom-call | tf_op jit(solution)/shard_map/jit(cholesky)/cholesky | solution.py:33
  149.0 9.8 %custom-call.33 = f32[1,128,128]{1,2,0:T(8,128)S(1)} custom-call(f32[1,128,128]{2,1,0:T(8,128)S(1)} %get-tuple-element.34), custom_call_target="InvertDiagBlocksLowerTriangular" | custom-call | tf_op jit(solution)/shard_map/jit(cholesky)/cholesky | solution.py:33
  159.0 1.3 convolution_subtract_fusion.2
  160.3 11.7 %cholesky.238 = f32[128,128]{1,0:T(8,128)S(1)} custom-call(f32[128,128]{1,0:T(8,128)S(1)} %cholesky.275), custom_call_target="Cholesky" | custom-call | tf_op jit(solution)/shard_map/jit(cholesky)/cholesky | solution.py:33
  172.8 9.8 %custom-call.34 = f32[1,128,128]{1,2,0:T(8,128)S(1)} custom-call(f32[1,128,128]{2,1,0:T(8,128)S(1)} %get-tuple-element.31), custom_call_target="InvertDiagBlocksLowerTriangular" | custom-call | tf_op jit(solution)/shard_map/jit(cholesky)/cholesky | solution.py:33
  184.2 11.7 %cholesky.255 = f32[128,128]{1,0:T(8,128)S(1)} custom-call(f32[128,128]{1,0:T(8,128)S(1)} %convolution_subtract_fusion.9), custom_call_target="Cholesky" | custom-call | tf_op jit(solution)/shard_map/jit(cholesky)/cholesky | solution.py:33
  199.9 1.6 fusion.1
  201.5 13.7 %while.1 = (s32[]{:T(128)}, f32[512,512]{1,0:T(8,128)}, s32[4,2]{0,1:T(2,128)S(1)}, f32[4,128,128]{2,1,0:T(8,128)}, s32[]{:T(128)}) while((s32[]{:T(128)}, f32[512,512]{1,0:T(8,128)}, s32[4,2]{0,1:T(2,128)S(1)}, f32[4,128,128]{2,1,0:T(8,128)}, s32[]{:T(128)}) %tuple.33), condition=%wide.while_cond, body=%wide.while_body.sunk | while | flops 2 | bytes 132705 | solution.py:34
  202.1 2.9 %bitcast_dynamic-update-slice_fusion.2 = f32[4,128,128]{2,1,0:T(8,128)} fusion(f32[4,128,128]{2,1,0:T(8,128)} %get-tuple-element.79, s32[]{:T(128)} %get-tuple-element.76, f32[512,512]{1,0:T(8,128)} %get-tuple-element.82, s32[]{:T(128)} %bitcast.58, s32[]{:T(128)} %bitcast.59), kind=kLoop, calls=%fused_computation.clone.1 | loop fusion | bytes 132608 | tf_op jit(solution)/shard_map/triangular_solve
  205.5 2.9 %bitcast_dynamic-update-slice_fusion.2 = f32[4,128,128]{2,1,0:T(8,128)} fusion(f32[4,128,128]{2,1,0:T(8,128)} %get-tuple-element.79, s32[]{:T(128)} %get-tuple-element.76, f32[512,512]{1,0:T(8,128)} %get-tuple-element.82, s32[]{:T(128)} %bitcast.58, s32[]{:T(128)} %bitcast.59), kind=kLoop, calls=%fused_computation.clone.1 | loop fusion | bytes 132608 | tf_op jit(solution)/shard_map/triangular_solve
  209.0 2.9 %bitcast_dynamic-update-slice_fusion.2 = f32[4,128,128]{2,1,0:T(8,128)} fusion(f32[4,128,128]{2,1,0:T(8,128)} %get-tuple-element.79, s32[]{:T(128)} %get-tuple-element.76, f32[512,512]{1,0:T(8,128)} %get-tuple-element.82, s32[]{:T(128)} %bitcast.58, s32[]{:T(128)} %bitcast.59), kind=kLoop, calls=%fused_computation.clone.1 | loop fusion | bytes 132608 | tf_op jit(solution)/shard_map/triangular_solve
  212.4 2.8 %bitcast_dynamic-update-slice_fusion.2 = f32[4,128,128]{2,1,0:T(8,128)} fusion(f32[4,128,128]{2,1,0:T(8,128)} %get-tuple-element.79, s32[]{:T(128)} %get-tuple-element.76, f32[512,512]{1,0:T(8,128)} %get-tuple-element.82, s32[]{:T(128)} %bitcast.58, s32[]{:T(128)} %bitcast.59), kind=kLoop, calls=%fused_computation.clone.1 | loop fusion | bytes 132608 | tf_op jit(solution)/shard_map/triangular_solve
  215.2 40.1 %custom-call.35 = f32[4,128,128]{1,2,0:T(8,128)S(1)} custom-call(f32[4,128,128]{2,1,0:T(8,128)} %get-tuple-element.10), custom_call_target="InvertDiagBlocksLowerTriangular" | custom-call | tf_op jit(solution)/shard_map/triangular_solve | solution.py:34
  262.4 1.3 convolution_subtract_fusion.3
  263.9 1.4 convolution_subtract_fusion.7
  265.5 1.7 convolution_subtract_fusion
  267.2 1.3 copy.7
  (78 shorter events, 18.3 us)
Async XLA Ops:
  7.2 58.3 %copy-start.5 = (f32[64,512]{1,0:T(8,128)S(1)}, f32[64,512]{1,0:T(8,128)}, u32[]{:S(2)}) copy-start(f32[64,512]{1,0:T(8,128)} %param.2) | copy-start | bytes 393220
  7.2 100.6 %all-reduce.4.cloned.1.call-start = ((), (), s32[]{:S(2)}) async-start(), calls=%async_computation | async-start | bytes 2621440 | tf_op jit(solution)/shard_map/psum | solution.py:32
  7.2 9.8 %collective-permute-start = (f32[64,512]{1,0:T(8,128)}, f32[64,512]{1,0:T(8,128)S(1)}, u32[]{:S(2)}, u32[]{:S(2)}) collective-permute-start(f32[64,512]{1,0:T(8,128)} %param.2), channel_id=1, source_target_pairs={{0,1},{1,2},{2,3},{3,4},{4,5},{5,6},{6,7},{7,0},{8,9},{9,10},{10,1... | collective-permute-start | bytes 393224 | tf_op jit(solution)/shard_map/ppermute | solution.py:18
  17.0 7.7 %collective-permute-start.1 = (f32[64,512]{1,0:T(8,128)S(1)}, f32[64,512]{1,0:T(8,128)S(1)}, u32[]{:S(2)}, u32[]{:S(2)}) collective-permute-start(f32[64,512]{1,0:T(8,128)S(1)} %collective-permute-done), channel_id=1, source_target_pairs={{0,1},{1,2},{2,3},{3,4},{4,5},{5,6},{6,7},{7,0},{8,9},{9,10},{10,1... | collective-permute-start | bytes 393224 | tf_op jit(solution)/shard_map/ppermute | solution.py:18
  24.7 7.7 %collective-permute-start.2 = (f32[64,512]{1,0:T(8,128)S(1)}, f32[64,512]{1,0:T(8,128)S(1)}, u32[]{:S(2)}, u32[]{:S(2)}) collective-permute-start(f32[64,512]{1,0:T(8,128)S(1)} %collective-permute-done.1), channel_id=1, source_target_pairs={{0,1},{1,2},{2,3},{3,4},{4,5},{5,6},{6,7},{7,0},{8,9},{9,10},{10,1... | collective-permute-start | bytes 393224 | tf_op jit(solution)/shard_map/ppermute | solution.py:18
  32.3 7.7 %collective-permute-start.3 = (f32[64,512]{1,0:T(8,128)S(1)}, f32[64,512]{1,0:T(8,128)S(1)}, u32[]{:S(2)}, u32[]{:S(2)}) collective-permute-start(f32[64,512]{1,0:T(8,128)S(1)} %collective-permute-done.2), channel_id=1, source_target_pairs={{0,1},{1,2},{2,3},{3,4},{4,5},{5,6},{6,7},{7,0},{8,9},{9,10},{10,1... | collective-permute-start | bytes 393224 | tf_op jit(solution)/shard_map/ppermute | solution.py:18
  40.0 7.7 %collective-permute-start.4 = (f32[64,512]{1,0:T(8,128)S(1)}, f32[64,512]{1,0:T(8,128)S(1)}, u32[]{:S(2)}, u32[]{:S(2)}) collective-permute-start(f32[64,512]{1,0:T(8,128)S(1)} %collective-permute-done.3), channel_id=1, source_target_pairs={{0,1},{1,2},{2,3},{3,4},{4,5},{5,6},{6,7},{7,0},{8,9},{9,10},{10,1... | collective-permute-start | bytes 393224 | tf_op jit(solution)/shard_map/ppermute | solution.py:18
  47.7 8.9 %collective-permute-start.5 = (f32[64,512]{1,0:T(8,128)S(1)}, f32[64,512]{1,0:T(8,128)S(1)}, u32[]{:S(2)}, u32[]{:S(2)}) collective-permute-start(f32[64,512]{1,0:T(8,128)S(1)} %collective-permute-done.4), channel_id=1, source_target_pairs={{0,1},{1,2},{2,3},{3,4},{4,5},{5,6},{6,7},{7,0},{8,9},{9,10},{10,1... | collective-permute-start | bytes 393224 | tf_op jit(solution)/shard_map/ppermute | solution.py:18
  56.5 7.7 %collective-permute-start.6 = (f32[64,512]{1,0:T(8,128)S(1)}, f32[64,512]{1,0:T(8,128)S(1)}, u32[]{:S(2)}, u32[]{:S(2)}) collective-permute-start(f32[64,512]{1,0:T(8,128)S(1)} %collective-permute-done.5), channel_id=1, source_target_pairs={{0,1},{1,2},{2,3},{3,4},{4,5},{5,6},{6,7},{7,0},{8,9},{9,10},{10,1... | collective-permute-start | bytes 393224 | tf_op jit(solution)/shard_map/ppermute | solution.py:18
  65.3 3.0 %copy-start.3 = (f32[512,128]{1,0:T(8,128)S(1)}, f32[512,128]{1,0:T(8,128)}, u32[]{:S(2)}) copy-start(f32[512,128]{1,0:T(8,128)} %param.3) | copy-start | bytes 786436
  107.8 2.6 copy-start
  111.9 1.0 copy-start.2
  184.2 71.1 %copy-start.6 = (f32[512,128]{1,0:T(8,128)S(1)}, f32[512,128]{1,0:T(8,128)}, u32[]{:S(2)}) copy-start(f32[512,128]{1,0:T(8,128)} %get-tuple-element.23) | copy-start | bytes 786436
  255.6 9.9 %copy-start.4 = (f32[512,128]{1,0:T(8,128)S(1)}, f32[512,128]{1,0:T(8,128)}, u32[]{:S(2)}) copy-start(f32[512,128]{1,0:T(8,128)} %param.3) | copy-start | bytes 786436
  260.3 6.9 %copy-start.1 = (f32[512,512]{0,1:T(8,128)S(1)}, f32[512,512]{0,1:T(8,128)}, u32[]{:S(2)}) copy-start(f32[512,512]{0,1:T(8,128)} %get-tuple-element.27) | copy-start | bytes 3145732
Sparse Core Ops, SparseCore 0:
  71.0 36.7 all-reduce.3
